TPU v7x, 32 devices: a whole 2x2x4 slice. The times are simulated.
32 devices in a mesh: grp: 4 (over y, x), tile: 8 (over z, core).
Axes of the slice: x: 2, y: 2, z: 4, core: 2. Of those that a mesh axis runs over, the one named last changes fastest.
Arguments:
- flow_fields: float32 [5, 256, 16, 128], P(None, 'tile', 'grp'), may hold values from -6 to 6
- turbulent_diffusivity: float32 [256, 16, 128], P('tile', 'grp'), may hold values from 0.05 to 0.3
- holder_unit: int32 [4, 256, 1], P('grp', 'tile'), may hold values from 0 to 7, as said below
- spray_volume_position: int32 [8, 1024, 128], P('tile'), may hold values from 0 to 511
- patch_pick_unreduced: int32 [8, 1024], P('tile'), may hold values from 0 to 1048575
- droplet_motion: float32 [8, 1024, 3, 128], P('tile'), may hold values from -6 to 6
- droplet_warmth: float32 [8, 1024, 128], P('tile'), may hold values from -6 to 6
- droplet_weightiness: float32 [8, 1024, 128], P('tile'), may hold values from 0.25 to 2
- droplet_multiplicity: float32 [8, 1024, 128], P('tile'), may hold values from 0.5 to 2
- living_spray_batches: int32 [8], P('tile'), may hold values from 1 to 1024, 4096 in all
Outputs:
- gas_next: float32 [5, 256, 16, 128], P(None, 'tile', 'grp')
Inputs may be any that keep to these rules, and one draw needn't show every extreme that they name: `holder_unit`: among the 32 tiles of one gas device (aligned blocks of 32 rows of owner, in order of its first two dimensions) no parcel device owns more than 8, and in every such block one parcel device owns exactly 8. Two parcel devices own no tile at all. Rows with g = 3 are not used. `living_spray_batches`: live blocks of a device are its first ones; the busiest parcel device has exactly 1024, and they sum to 4096.
All inputs are finite; a program needn't handle non-finite values.
Results may differ from a plain program's by a relative error of at most 0.0045.
Values may be sent and summed in bfloat16 or wider, within the bound.
A program may use at most 64 MiB of HBM per device.

v0:
```python
import functools

import jax
import jax.numpy as jnp
from jax import lax
from jax.experimental import pallas as pl
from jax.experimental.pallas import tpu as pltpu
from jax.sharding import PartitionSpec as P

MESH = pl.DeviceIdType.MESH
SLOTS = 8
BATCH = 32
VMEM = pl.BlockSpec(memory_space=pltpu.VMEM)
SMEM = pl.BlockSpec(memory_space=pltpu.SMEM)
F32, BF16, I32 = jnp.float32, jnp.bfloat16, jnp.int32


def pack_kernel(ng, owners, own_ref, flow_ref, nu_ref, send_ref, sel_ref, gas_ref, low_ref, first_ref, last_ref, nut_ref):
    nf, planes, rows_y, width = flow_ref.shape
    gas_side = lax.axis_index("grp") < ng - 1
    row = jnp.broadcast_to(own_ref[0], (128, 128))
    col = row.T
    s = lax.broadcasted_iota(I32, (128, 128), 0)
    l = lax.broadcasted_iota(I32, (128, 128), 1)
    earlier = jnp.where((col == row) & (s < l), 1, 0)
    rank = jnp.sum(earlier, axis=0, keepdims=True)
    goal = (own_ref[0] * SLOTS + rank)[:, 0:planes]
    target = lax.broadcasted_iota(I32, (owners * SLOTS, planes), 0)
    sel = jnp.where(goal == target, 1.0, 0.0).astype(BF16)
    sel_ref[...] = sel
    rows = nf * rows_y
    for r in range(0, rows, 2):
        pair = []
        for q in (r, r + 1):
            cells = jnp.where(gas_side, flow_ref[q % nf, :, q // nf, :], 0.0)
            gas_ref[q] = cells
            low = cells.astype(BF16)
            low_ref[q] = low
            pair.append(jnp.dot(sel, low, preferred_element_type=F32))
        for o in range(owners):
            lo, hi = o * SLOTS, (o + 1) * SLOTS
            both = jnp.concatenate([pair[0][lo:hi], pair[1][lo:hi]], axis=0).astype(BF16)
            send_ref[o, r * SLOTS : (r + 2) * SLOTS, :] = both
    for y in range(rows_y):
        nut_ref[y] = nu_ref[:, y, :]
    first_ref[...] = gas_ref[:, 0, :].astype(BF16)
    last_ref[...] = gas_ref[:, planes - 1, :].astype(BF16)


def greet(peers):
    barrier = pltpu.get_barrier_semaphore()
    for peer in peers:
        pl.semaphore_signal(barrier, inc=1, device_id=peer, device_id_type=MESH)
    pl.semaphore_wait(barrier, len(peers))


def exchange_kernel(
    ng, nt, nf, send_ref, gas_ref, first_ref, last_ref, own_ref,
    recv_ref, ylo_ref, yhi_ref, xlo_ref, xhi_ref, all_ref,
    tile_s, tile_r, own_s, own_r, own2_s, own2_r, halo_s, halo_r, local_sem,
):
    g, t = lax.axis_index("grp"), lax.axis_index("tile")
    grp_peers = [(lax.rem(g + k, ng), t) for k in range(1, ng)]
    tile_peers = [(g, lax.rem(t + k, nt)) for k in range(1, nt)]
    greet(grp_peers + tile_peers)

    def copy(src, dst, ss, rs, dev):
        c = pltpu.make_async_remote_copy(
            src_ref=src, dst_ref=dst, send_sem=ss, recv_sem=rs, device_id=dev, device_id_type=MESH
        )
        c.start()
        return c

    own_copies = [
        copy(own_ref.at[0], all_ref.at[t, g], own_s.at[k], own_r.at[k], peer)
        for k, peer in enumerate(grp_peers)
    ]
    mine = pltpu.make_async_copy(own_ref.at[0], all_ref.at[t, g], local_sem.at[0])
    mine.start()
    slab = pltpu.make_async_copy(send_ref.at[t], recv_ref.at[t], local_sem.at[1])
    slab.start()
    rows = gas_ref.shape[0]
    others = [
        copy(gas_ref.at[pl.ds(rows - nf, nf)], ylo_ref, halo_s.at[0], halo_r.at[0], grp_peers[0]),
        copy(gas_ref.at[pl.ds(0, nf)], yhi_ref, halo_s.at[1], halo_r.at[1], grp_peers[-1]),
        copy(last_ref, xlo_ref, halo_s.at[2], halo_r.at[2], tile_peers[0]),
        copy(first_ref, xhi_ref, halo_s.at[3], halo_r.at[3], tile_peers[-1]),
    ]
    for k, peer in enumerate(tile_peers):
        others.append(copy(send_ref.at[peer[1]], recv_ref.at[t], tile_s.at[k], tile_r.at[k], peer))
    mine.wait()
    for c in own_copies:
        c.wait()
    for k, peer in enumerate(tile_peers):
        others.append(copy(all_ref.at[t], all_ref.at[t], own2_s.at[k], own2_r.at[k], peer))
    slab.wait()
    for c in others:
        c.wait()


def parcel_kernel(
    ng, nt, nf, scal_ref, recv_ref, own_ref, pick_ref, pos_ref, mot_ref, warm_ref, mass_ref, mult_ref,
    dep_ref,
    stage, table, acc, seen, par, src, hot, ints, smem, sem,
):
    g, p, live = lax.axis_index("grp"), lax.axis_index("tile"), scal_ref[0]
    slots = nt * SLOTS
    blocks = pos_ref.shape[0]
    shift = blocks.bit_length() - 1
    prow = blocks // 128
    owned = jnp.where(own_ref[...] == p, 1, 0)
    counts = jnp.sum(owned, axis=1, keepdims=True)
    which = lax.broadcasted_iota(I32, counts.shape, 0)
    counts = jnp.where(lax.rem(which, ng) < ng - 1, counts, 0)
    total = jnp.maximum(jnp.sum(counts, axis=0, keepdims=True), 1)
    pick = pick_ref[...]
    total_f = total.astype(F32)
    quotient = jnp.floor(pick.astype(F32) / total_f).astype(I32)
    left = pick - quotient * total
    left = jnp.where(left < 0, left + total, left)
    left = jnp.where(left >= total, left - total, left)
    group = lax.rem(which, ng)
    low = jnp.sum(jnp.where(group < g, counts, 0), axis=0, keepdims=True)
    mine = jnp.sum(jnp.where(group == g, counts, 0), axis=0, keepdims=True)
    inner = left - low
    slot = inner
    passed = jnp.zeros((1, 1), I32)
    for d in range(nt - 1):
        count = jnp.sum(jnp.where(which == d * ng + g, counts, 0), axis=0, keepdims=True)
        passed = passed + count
        slot = slot + jnp.where(inner >= passed, SLOTS - count, 0)
    row = lax.broadcasted_iota(I32, (prow, 128), 0)
    lane = lax.broadcasted_iota(I32, (prow, 128), 1)
    number = row * 128 + lane
    inside = (inner >= 0) & (inner < mine) & (number < live)
    flags = jnp.where(inside, 1, 0)
    square_a = lax.broadcasted_iota(I32, (128, 128), 0)
    square_b = lax.broadcasted_iota(I32, (128, 128), 1)
    before = jnp.where(square_a < square_b, 1.0, 0.0).astype(BF16)
    flags_low = flags.astype(F32).astype(BF16)
    place = jnp.dot(flags_low, before, preferred_element_type=F32).astype(I32)
    sums = jnp.sum(flags, axis=1, keepdims=True)
    start = jnp.zeros((1, 1), I32)
    listed = jnp.zeros((3 * prow, 128), F32)
    lane_f, slot_f = lane[0:1].astype(F32), slot.astype(F32)
    for i in range(prow):
        at = jnp.where(inside[i : i + 1], place[i : i + 1] + start, -1)
        goes = row == (at >> 7)
        parts = [
            jnp.where(goes, v, 0.0) for v in (slot_f[i : i + 1], jnp.full((1, 128), float(i), F32), lane_f)
        ]
        spot = jnp.where(square_a == (at & 127), 1.0, 0.0).astype(BF16)
        listed += lax.dot_general(
            jnp.concatenate(parts, axis=0).astype(BF16), spot, (((1,), (1,)), ((), ())),
            preferred_element_type=F32,
        )
        start = start + sums[i : i + 1]
    listed = listed.astype(I32)
    entry = (listed[0:prow] << shift) + listed[prow : 2 * prow] * 128 + listed[2 * prow :]
    ints[0:prow, :] = jnp.where(number < start, entry, slots << shift)
    ints[prow : prow + 8, :] = jnp.broadcast_to(start, (8, 128))
    to_smem = pltpu.make_async_copy(ints, smem, sem)
    to_smem.start()
    rows = recv_ref.shape[1] // SLOTS
    stage[...] = jnp.zeros_like(stage)
    for d in range(nt):
        for r in range(0, rows, 2):
            both = recv_ref[d, r * SLOTS : (r + 2) * SLOTS, :].astype(F32)
            for h in range(2):
                row = (r + h) // nf * 8 + (r + h) % nf
                stage[pl.ds(d * SLOTS * 32 + row, SLOTS, stride=32), :] = both[h * SLOTS : (h + 1) * SLOTS]

    @pl.loop(0, slots + 1)
    def _(i):
        table[i] = stage[pl.ds(pl.multiple_of(i * 32, 32), 32), :].astype(BF16)

    acc[...] = jnp.zeros_like(acc)
    src[...] = jnp.zeros_like(src)
    to_smem.wait()

    n = smem[prow, 0]
    sub = lax.broadcasted_iota(I32, (128, 128), 0).astype(F32).astype(BF16)
    yes, no = jnp.ones((128, 128), BF16), jnp.zeros((128, 128), BF16)

    @pl.loop(0, (n + BATCH - 1) // BATCH)
    def _(step):
        where_at, ys = [], []
        for j in range(BATCH):
            v = smem[step // (128 // BATCH), lax.rem(step, 128 // BATCH) * BATCH + j]
            b = v & (blocks - 1)
            slot = v >> shift
            cell = pos_ref[pl.ds(b, 1), :]
            y = cell >> 7
            z = (cell & 127).astype(F32).astype(BF16)
            one = jnp.where(sub == jnp.broadcast_to(z, (128, 128)), yes, no)
            hot[j] = one
            got = jnp.dot(table[slot], one, preferred_element_type=F32)
            upper = jnp.where(y < 1, got[0:8], got[8:16])
            lower = jnp.where(y < 3, got[16:24], got[24:32])
            seen[pl.ds(j * 8, 8), :] = jnp.where(y < 2, upper, lower)
            for f in range(3):
                par[f : f + 1, j, :] = mot_ref[f, pl.ds(b, 1), :]
            par[3:4, j, :] = warm_ref[pl.ds(b, 1), :]
            par[4:5, j, :] = mass_ref[pl.ds(b, 1), :]
            par[5:6, j, :] = mult_ref[pl.ds(b, 1), :]
            where_at.append(slot)
            ys.append(y)
        field = [seen[pl.ds(f, BATCH, stride=8), :] for f in range(5)]
        v0, v1, v2, warm, mass, mult = [par[f] for f in range(6)]
        r0, r1, r2 = field[0] - v0, field[1] - v1, field[2] - v2
        speed_sq = r0 * r0 + r1 * r1 + r2 * r2
        inv_surface = jnp.exp(jnp.log(mass) * (-2.0 / 3.0))
        inverse_tau = 0.8 * (1.0 + 0.15 * jnp.exp(0.3435 * jnp.log(1.0 + speed_sq))) * inv_surface
        relax = 1.0 - jnp.exp(-0.5 * inverse_tau)
        heating = 1.0 / (1.0 + jnp.exp(field[4] - field[3]))
        remain = jnp.exp(-0.3 * heating * inv_surface)
        new_mass = mass * remain
        warming = 1.0 - jnp.exp(-0.25 * inverse_tau)
        new_warm = warm + warming * (field[3] - warm) - 0.5 * (1.0 - remain)
        outs = [mass * v - new_mass * (v + relax * r) for v, r in ((v0, r0), (v1, r1), (v2, r2))]
        outs += [mass * warm - new_mass * new_warm, mass - new_mass]
        for f, o in enumerate(outs):
            src[pl.ds(f, BATCH, stride=8), :] = mult * o
        added = []
        for j in range(BATCH):
            s8 = src[pl.ds(j * 8, 8), :]
            s32 = jnp.concatenate([jnp.where(ys[j] == k, s8, 0.0) for k in range(4)], axis=0).astype(BF16)
            added.append(
                lax.dot_general(s32, hot[j], (((1,), (1,)), ((), ())), preferred_element_type=F32)
            )
        for j in range(BATCH):
            at = pl.ds(pl.multiple_of(where_at[j] * 32, 32), 32)
            acc[at, :] = acc[at, :] + added[j]

    for d in range(nt):
        for r in range(0, rows, 2):
            pair = [
                acc[pl.ds(d * SLOTS * 32 + q // nf * 8 + q % nf, SLOTS, stride=32), :] for q in (r, r + 1)
            ]
            dep_ref[d, r * SLOTS : (r + 2) * SLOTS, :] = jnp.concatenate(pair, axis=0).astype(BF16)


def finish_kernel(
    ng, nt, nf, dep_ref, selt_ref, gas_ref, nu_ref, ylo_ref, yhi_ref, xlo_ref, xhi_ref,
    out_ref, recv, part, tile_s, tile_r, local_sem,
):
    g, t = lax.axis_index("grp"), lax.axis_index("tile")
    peers = [(g, lax.rem(t + k, nt)) for k in range(1, nt)]
    greet(peers)
    copies = []
    for k, peer in enumerate(peers):
        c = pltpu.make_async_remote_copy(
            src_ref=dep_ref.at[peer[1]], dst_ref=recv.at[t], send_sem=tile_s.at[k],
            recv_sem=tile_r.at[k], device_id=peer, device_id_type=MESH,
        )
        c.start()
        copies.append(c)
    slab = pltpu.make_async_copy(dep_ref.at[t], recv.at[t], local_sem)
    slab.start()
    rows, planes, width = gas_ref.shape
    sub = lax.broadcasted_iota(I32, (planes, width), 0)
    lane = lax.broadcasted_iota(I32, (planes, width), 1)
    gas_side = jnp.where(g < ng - 1, 1.0, 0.0).astype(F32)
    has_low = jnp.where(t > 0, 1.0, 0.0).astype(F32)
    has_high = jnp.where(t < nt - 1, 1.0, 0.0).astype(F32)
    x_low = xlo_ref[...].astype(F32) * has_low
    x_high = xhi_ref[...].astype(F32) * has_high
    for r in range(rows):
        mid = gas_ref[r]
        below = gas_ref[r - nf] if r >= nf else ylo_ref[r].astype(F32)
        above = gas_ref[r + nf] if r < rows - nf else yhi_ref[r - (rows - nf)].astype(F32)
        total = below + above
        total += jnp.where(sub == 0, x_low[r : r + 1], pltpu.roll(mid, 1, 0))
        total += jnp.where(sub == planes - 1, x_high[r : r + 1], pltpu.roll(mid, planes - 1, 0))
        total += jnp.where(lane == 0, 0.0, pltpu.roll(mid, 1, 1))
        total += jnp.where(lane == width - 1, 0.0, pltpu.roll(mid, width - 1, 1))
        part[r] = (mid + 0.5 * nu_ref[r // nf] * (total - 6.0 * mid)) * gas_side
    slab.wait()
    for c in copies:
        c.wait()
    selt = selt_ref[...]
    for r in range(0, rows, 2):
        both = recv[:, r * SLOTS : (r + 2) * SLOTS, :].astype(F32)
        for h in range(2):
            inc = both[:, h * SLOTS : (h + 1) * SLOTS, :].reshape(nt * SLOTS, width).astype(BF16)
            placed = lax.dot_general(
                selt, inc, (((0,), (0,)), ((), ())), preferred_element_type=F32
            )
            q = r + h
            out_ref[q % nf, :, q // nf, :] = part[q] + placed * gas_side


def local(
    flow_fields, turbulent_diffusivity, holder_unit, spray_volume_position, patch_pick_unreduced,
    droplet_motion, droplet_warmth, droplet_weightiness, droplet_multiplicity, living_spray_batches,
):
    ng, nt = lax.axis_size("grp"), lax.axis_size("tile")
    nf, planes, rows_y, width = flow_fields.shape
    rows = nf * rows_y
    own_row = jnp.pad(holder_unit.reshape(1, 1, planes), ((0, 0), (0, 0), (0, 128 - planes)), constant_values=-1)
    slab = jax.ShapeDtypeStruct((nt, rows * SLOTS, width), BF16)
    slab_bytes = nt * rows * SLOTS * width * 2
    dma = pltpu.SemaphoreType.DMA
    edge = jax.ShapeDtypeStruct((rows, width), BF16)
    send, sel, gas, gas_low, first, last, nu = pl.pallas_call(
        functools.partial(pack_kernel, ng, nt),
        out_shape=(
            slab,
            jax.ShapeDtypeStruct((nt * SLOTS, planes), BF16),
            jax.ShapeDtypeStruct((rows, planes, width), F32),
            jax.ShapeDtypeStruct((rows, planes, width), BF16),
            edge,
            edge,
            jax.ShapeDtypeStruct((rows_y, planes, width), F32),
        ),
        in_specs=[VMEM] * 3, out_specs=(VMEM,) * 7,
        compiler_params=pltpu.CompilerParams(vmem_limit_bytes=slab_bytes * 2 + (6 << 20)),
        name="pack",
    )(own_row, flow_fields, turbulent_diffusivity)
    halo_y = jax.ShapeDtypeStruct((nf, planes, width), BF16)
    halo_x = jax.ShapeDtypeStruct((rows, width), BF16)
    recv, ylo, yhi, xlo, xhi, own_all = pl.pallas_call(
        functools.partial(exchange_kernel, ng, nt, nf),
        out_shape=(slab, halo_y, halo_y, halo_x, halo_x, jax.ShapeDtypeStruct((nt, ng, 1, 128), I32)),
        in_specs=[VMEM] * 5, out_specs=(VMEM,) * 6,
        scratch_shapes=[
            dma((nt - 1,)), dma((nt - 1,)), dma((ng - 1,)), dma((ng - 1,)),
            dma((nt - 1,)), dma((nt - 1,)), dma((4,)), dma((4,)), dma((2,)),
        ],
        compiler_params=pltpu.CompilerParams(collective_id=0, has_side_effects=True, vmem_limit_bytes=slab_bytes * 2 + (6 << 20)),
        name="exchange",
    )(send, gas_low, first, last, own_row)
    blocks = spray_volume_position.shape[1]
    slots = nt * SLOTS
    prow = blocks // 128
    dep = pl.pallas_call(
        functools.partial(parcel_kernel, ng, nt, nf),
        out_shape=slab,
        in_specs=[SMEM] + [VMEM] * 8, out_specs=VMEM,
        scratch_shapes=[
            pltpu.VMEM(((slots + 1) * 32, width), F32),
            pltpu.VMEM((slots + 1, 32, width), BF16),
            pltpu.VMEM(((slots + 1) * 32, width), F32),
            pltpu.VMEM((BATCH * 8, width), F32),
            pltpu.VMEM((6, BATCH, width), F32),
            pltpu.VMEM((BATCH * 8, width), F32),
            pltpu.VMEM((BATCH, 128, 128), BF16),
            pltpu.VMEM((prow + 8, 128), I32),
            pltpu.SMEM((prow + 8, 128), I32),
            dma,
        ],
        compiler_params=pltpu.CompilerParams(vmem_limit_bytes=slab_bytes * 12 + (8 << 20)),
        name="parcels",
    )(
        living_spray_batches, recv, own_all.reshape(nt * ng, 128), patch_pick_unreduced.reshape(prow, 128),
        spray_volume_position[0], droplet_motion[0].transpose(1, 0, 2), droplet_warmth[0], droplet_weightiness[0],
        droplet_multiplicity[0],
    )
    return pl.pallas_call(
        functools.partial(finish_kernel, ng, nt, nf),
        out_shape=jax.ShapeDtypeStruct((nf, planes, rows_y, width), F32),
        in_specs=[VMEM] * 8, out_specs=VMEM,
        scratch_shapes=[
            pltpu.VMEM((nt, rows * SLOTS, width), BF16), pltpu.VMEM((rows, planes, width), F32),
            dma((nt - 1,)), dma((nt - 1,)), dma,
        ],
        compiler_params=pltpu.CompilerParams(collective_id=1, has_side_effects=True, vmem_limit_bytes=slab_bytes * 2 + (6 << 20)),
        name="finish",
    )(dep, sel, gas, nu, ylo, yhi, xlo, xhi)


def solution(mesh):
    in_specs = (
        P(None, "tile", "grp", None),
        P("tile", "grp", None),
        P("grp", "tile", None),
        P("tile", None, None),
        P("tile", None),
        P("tile", None, None, None),
        P("tile", None, None),
        P("tile", None, None),
        P("tile", None, None),
        P("tile"),
    )
    out_specs = P(None, "tile", "grp", None)
    return jax.shard_map(local, mesh=mesh, in_specs=in_specs, out_specs=out_specs, check_vma=False)
```

profile of v0, /device:TPU:1, one launch (start us, length us, event | category | flops | bytes accessed | tf_op | source)
XLA Modules:
  0.0 50.0 jit_solution(14734812625550850677)
XLA Ops:
  0.0 0.7 %pad.4.own_ref = s32[1,1,128]{2,1,0:T(1,128)S(1)} pad(s32[1,1,32]{2,1,0:T(1,128)} %bitcast.17, s32[]{:T(128)} %constant.0.clone.1), padding=0_0x0_0x0_96 | pad | bytes 644 | tf_op jit(solution)/shard_map/jit(_pad)/pad | solution.py:300
  0.7 0.0 copy-start.5
  0.7 1.0 %copy-done.5 = f32[5,32,4,128]{3,2,1,0:T(4,128)S(1)} copy-done((f32[5,32,4,128]{3,2,1,0:T(4,128)S(1)}, f32[5,32,4,128]{3,2,1,0:T(4,128)}, u32[]{:S(2)}) %copy-start.5) | copy-done | bytes 327704
  1.6 0.0 copy-start.6
  1.6 0.8 %copy-done.6 = f32[32,4,128]{2,1,0:T(4,128)S(1)} copy-done((f32[32,4,128]{2,1,0:T(4,128)S(1)}, f32[32,4,128]{2,1,0:T(4,128)}, u32[]{:S(2)}) %copy-start.6) | copy-done | bytes 65560
  2.5 0.8 %pack.1 = (bf16[8,160,128]{2,1,0:T(8,128)(2,1)S(1)}, bf16[64,32]{1,0:T(8,128)(2,1)S(1)}, f32[20,32,128]{2,1,0:T(8,128)S(1)}, bf16[20,32,128]{2,1,0:T(8,128)(2,1)...) custom-call(s32[1,1,128]{2,1,0:T(1,128)S(1)} %pad.4.own_ref, ...), custom_call_target="tpu_custom_call" | custom-call | tf_op jit(solution)/shard_map/pack/pallas_call | solution.py:305
  3.3 14.5 %exchange.1 = (bf16[8,160,128]{2,1,0:T(8,128)(2,1)S(1)}, bf16[5,32,128]{2,1,0:T(8,128)(2,1)S(1)}, bf16[5,32,128]{2,1,0:T(8,128)(2,1)S(1)}, bf16[20,128]{1,0:T(8,...) custom-call(bf16[8,160,128]{2,1,0:T(8,128)(2,1)S(1)} %get-tuple-element.18.send_ref, ...), custom_call_target="tpu_custom_call" | custom-call | tf_op jit(solution)/shard_map/exchange/pallas_call | solution.py:322
  18.5 0.0 copy-start
  18.5 1.4 %copy-done = f32[1,1024,3,128]{3,1,2,0:T(8,128)S(1)} copy-done((f32[1,1024,3,128]{3,1,2,0:T(8,128)S(1)}, f32[1,1024,3,128]{3,1,2,0:T(8,128)}, u32[]{:S(2)}) %copy-start) | copy-done | bytes 1572888
  19.9 0.0 copy-start.1
  19.9 1.0 %copy-done.1 = s32[1,1024,128]{2,1,0:T(8,128)S(1)} copy-done((s32[1,1024,128]{2,1,0:T(8,128)S(1)}, s32[1,1024,128]{2,1,0:T(8,128)}, u32[]{:S(2)}) %copy-start.1) | copy-done | bytes 524312
  20.9 0.0 copy-start.2
  20.9 1.0 %copy-done.2 = f32[1,1024,128]{2,1,0:T(8,128)S(1)} copy-done((f32[1,1024,128]{2,1,0:T(8,128)S(1)}, f32[1,1024,128]{2,1,0:T(8,128)}, u32[]{:S(2)}) %copy-start.2) | copy-done | bytes 524312
  21.9 0.0 copy-start.3
  21.9 1.0 %copy-done.3 = f32[1,1024,128]{2,1,0:T(8,128)S(1)} copy-done((f32[1,1024,128]{2,1,0:T(8,128)S(1)}, f32[1,1024,128]{2,1,0:T(8,128)}, u32[]{:S(2)}) %copy-start.3) | copy-done | bytes 524312
  23.0 0.0 copy-start.4
  23.0 1.0 %copy-done.4 = f32[1,1024,128]{2,1,0:T(8,128)S(1)} copy-done((f32[1,1024,128]{2,1,0:T(8,128)S(1)}, f32[1,1024,128]{2,1,0:T(8,128)}, u32[]{:S(2)}) %copy-start.4) | copy-done | bytes 524312
  24.0 0.0 copy-start.7
  24.0 0.7 %copy-done.7 = s32[1,1024]{1,0:T(1,128)S(1)} copy-done((s32[1,1024]{1,0:T(1,128)S(1)}, s32[1,1024]{1,0:T(1,128)}, u32[]{:S(2)}) %copy-start.7) | copy-done | bytes 4120
  24.7 5.1 %parcels.1.dep_ref = bf16[8,160,128]{2,1,0:T(8,128)(2,1)S(1)} custom-call(s32[1]{0:T(128)S(6)} %copy.12.scal_ref, bf16[8,160,128]{2,1,0:T(8,128)(2,1)S(1)} %get-tuple-element.22.recv_ref, s32[32,128]{1,0:T(8,128)S(1)} %bitcast.15, s32[8,128]{1,0:T(8,128)S(1)} %bitcast.16, s32[1024,128]{1,0:T(8,128)S(1)} %bitcast.11, f32[3,1024,128]{2,1,0:T(8,128)S(1)} %bitcast.10, ...), custom_call_target="tpu_custom_call" | custom-call | tf_op jit(solution)/shard_map/parcels/pallas_call | solution.py:336
  29.9 19.4 %finish.1 = f32[5,32,4,128]{3,2,1,0:T(4,128)S(1)} custom-call(bf16[8,160,128]{2,1,0:T(8,128)(2,1)S(1)} %parcels.1.dep_ref, bf16[64,32]{1,0:T(8,128)(2,1)S(1)} %get-tuple-element.24.selt_ref, f32[20,32,128]{2,1,0:T(8,128)S(1)} %get-tuple-element.25.gas_ref, f32[4,32,128]{2,1,0:T(8,128)S(1)} %get-tuple-element.26.nu_ref, ...), custom_call_target="tpu_custom_call" | custom-call | tf_op jit(solution)/shard_map/finish/pallas_call | solution.py:359
  49.2 0.7 %copy.13 = f32[5,32,4,128]{3,2,1,0:T(4,128)} copy(f32[5,32,4,128]{3,2,1,0:T(4,128)S(1)} %finish.1) | data formatting | bytes 655360
Async XLA Ops:
  0.7 1.0 %copy-start.5 = (f32[5,32,4,128]{3,2,1,0:T(4,128)S(1)}, f32[5,32,4,128]{3,2,1,0:T(4,128)}, u32[]{:S(2)}) copy-start(f32[5,32,4,128]{3,2,1,0:T(4,128)} %flow_ref.1) | copy-start | bytes 983044
  1.6 0.8 %copy-start.6 = (f32[32,4,128]{2,1,0:T(4,128)S(1)}, f32[32,4,128]{2,1,0:T(4,128)}, u32[]{:S(2)}) copy-start(f32[32,4,128]{2,1,0:T(4,128)} %nu_ref.1) | copy-start | bytes 196612
  18.5 1.4 %copy-start = (f32[1,1024,3,128]{3,1,2,0:T(8,128)S(1)}, f32[1,1024,3,128]{3,1,2,0:T(8,128)}, u32[]{:S(2)}) copy-start(f32[1,1024,3,128]{3,1,2,0:T(8,128)} %param.15) | copy-start | bytes 4718596
  19.9 1.0 %copy-start.1 = (s32[1,1024,128]{2,1,0:T(8,128)S(1)}, s32[1,1024,128]{2,1,0:T(8,128)}, u32[]{:S(2)}) copy-start(s32[1,1024,128]{2,1,0:T(8,128)} %param.13) | copy-start | bytes 1572868
  20.9 1.0 %copy-start.2 = (f32[1,1024,128]{2,1,0:T(8,128)S(1)}, f32[1,1024,128]{2,1,0:T(8,128)}, u32[]{:S(2)}) copy-start(f32[1,1024,128]{2,1,0:T(8,128)} %param.16) | copy-start | bytes 1572868
  21.9 1.0 %copy-start.3 = (f32[1,1024,128]{2,1,0:T(8,128)S(1)}, f32[1,1024,128]{2,1,0:T(8,128)}, u32[]{:S(2)}) copy-start(f32[1,1024,128]{2,1,0:T(8,128)} %param.17) | copy-start | bytes 1572868
  23.0 1.0 %copy-start.4 = (f32[1,1024,128]{2,1,0:T(8,128)S(1)}, f32[1,1024,128]{2,1,0:T(8,128)}, u32[]{:S(2)}) copy-start(f32[1,1024,128]{2,1,0:T(8,128)} %param.18) | copy-start | bytes 1572868
  24.0 0.7 %copy-start.7 = (s32[1,1024]{1,0:T(1,128)S(1)}, s32[1,1024]{1,0:T(1,128)}, u32[]{:S(2)}) copy-start(s32[1,1024]{1,0:T(1,128)} %param.14) | copy-start | bytes 12292
where the time goes:
time: 49.4 us; the launch traced here: 50 us
  Pallas kernels  39.8 us (81%)
  local copies, waits for them, and re-layouts  9.45 us (19%)
  between operations  0.7 us (1%)
    pallas_call x1, Pallas kernels, local(): pl.pallas_call(functools.partial(finish_kernel, ng, nt, nf), out_shape=ja...  19.4 us
    pallas_call x1, Pallas kernels, local(): pl.pallas_call(functools.partial(exchange_kernel, ng, nt, nf), out_shape=...  14.5 us
    unnamed x17, local copies, waits for them, and re-layouts  8.79 us
    pallas_call x1, Pallas kernels, local(): pl.pallas_call(functools.partial(parcel_kernel, ng, nt, nf), out_shape=sl...  5.12 us

commit v1 on v0

--- a/solution.py
+++ b/solution.py
@@ -10,21 +10,25 @@
 MESH = pl.DeviceIdType.MESH
 SLOTS = 8
 BATCH = 32
+HBM = pl.BlockSpec(memory_space=pltpu.MemorySpace.HBM)
 VMEM = pl.BlockSpec(memory_space=pltpu.VMEM)
 SMEM = pl.BlockSpec(memory_space=pltpu.SMEM)
 F32, BF16, I32 = jnp.float32, jnp.bfloat16, jnp.int32
 
 
-def pack_kernel(ng, owners, own_ref, flow_ref, nu_ref, send_ref, sel_ref, gas_ref, low_ref, first_ref, last_ref, nut_ref):
+def pack_kernel(ng, owners, holder_ref, flow_ref, send_ref, sel_ref, gas_ref, low_ref, first_ref, last_ref, padded_ref):
     nf, planes, rows_y, width = flow_ref.shape
     gas_side = lax.axis_index("grp") < ng - 1
-    row = jnp.broadcast_to(own_ref[0], (128, 128))
+    padded_ref[0] = jnp.full((1, 128), -1, I32)
+    padded_ref[0, :, 0:planes] = holder_ref[...]
+    own = padded_ref[0]
+    row = jnp.broadcast_to(own, (128, 128))
     col = row.T
     s = lax.broadcasted_iota(I32, (128, 128), 0)
     l = lax.broadcasted_iota(I32, (128, 128), 1)
     earlier = jnp.where((col == row) & (s < l), 1, 0)
     rank = jnp.sum(earlier, axis=0, keepdims=True)
-    goal = (own_ref[0] * SLOTS + rank)[:, 0:planes]
+    goal = (own * SLOTS + rank)[:, 0:planes]
     target = lax.broadcasted_iota(I32, (owners * SLOTS, planes), 0)
     sel = jnp.where(goal == target, 1.0, 0.0).astype(BF16)
     sel_ref[...] = sel
@@ -41,8 +45,6 @@
             lo, hi = o * SLOTS, (o + 1) * SLOTS
             both = jnp.concatenate([pair[0][lo:hi], pair[1][lo:hi]], axis=0).astype(BF16)
             send_ref[o, r * SLOTS : (r + 2) * SLOTS, :] = both
-    for y in range(rows_y):
-        nut_ref[y] = nu_ref[:, y, :]
     first_ref[...] = gas_ref[:, 0, :].astype(BF16)
     last_ref[...] = gas_ref[:, planes - 1, :].astype(BF16)
 
@@ -99,11 +101,16 @@
 
 
 def parcel_kernel(
-    ng, nt, nf, scal_ref, recv_ref, own_ref, pick_ref, pos_ref, mot_ref, warm_ref, mass_ref, mult_ref,
+    ng, nt, nf, scal_ref, recv_ref, own_ref, pick_ref, pos_hbm, mot_hbm, warm_hbm, mass_hbm, mult_hbm,
     dep_ref,
-    stage, table, acc, seen, par, src, hot, ints, smem, sem,
+    pos_ref, mot_ref, warm_ref, mass_ref, mult_ref, load_sem, stage, table, acc, seen, par, src, hot, ints, smem, sem,
 ):
     g, p, live = lax.axis_index("grp"), lax.axis_index("tile"), scal_ref[0]
+    pairs = [(pos_hbm, pos_ref), (warm_hbm, warm_ref), (mass_hbm, mass_ref), (mult_hbm, mult_ref)]
+    pairs += [(mot_hbm.at[f], mot_ref.at[f]) for f in range(3)]
+    loads = [pltpu.make_async_copy(a, b, load_sem.at[k]) for k, (a, b) in enumerate(pairs)]
+    for c in loads:
+        c.start()
     slots = nt * SLOTS
     blocks = pos_ref.shape[0]
     shift = blocks.bit_length() - 1
@@ -179,6 +186,8 @@
     to_smem.wait()
 
     n = smem[prow, 0]
+    for c in loads:
+        c.wait()
     sub = lax.broadcasted_iota(I32, (128, 128), 0).astype(F32).astype(BF16)
     yes, no = jnp.ones((128, 128), BF16), jnp.zeros((128, 128), BF16)
 
@@ -274,7 +283,7 @@
         total += jnp.where(sub == planes - 1, x_high[r : r + 1], pltpu.roll(mid, planes - 1, 0))
         total += jnp.where(lane == 0, 0.0, pltpu.roll(mid, 1, 1))
         total += jnp.where(lane == width - 1, 0.0, pltpu.roll(mid, width - 1, 1))
-        part[r] = (mid + 0.5 * nu_ref[r // nf] * (total - 6.0 * mid)) * gas_side
+        part[r] = (mid + 0.5 * nu_ref[:, r // nf, :] * (total - 6.0 * mid)) * gas_side
     slab.wait()
     for c in copies:
         c.wait()
@@ -297,12 +306,11 @@
     ng, nt = lax.axis_size("grp"), lax.axis_size("tile")
     nf, planes, rows_y, width = flow_fields.shape
     rows = nf * rows_y
-    own_row = jnp.pad(holder_unit.reshape(1, 1, planes), ((0, 0), (0, 0), (0, 128 - planes)), constant_values=-1)
     slab = jax.ShapeDtypeStruct((nt, rows * SLOTS, width), BF16)
     slab_bytes = nt * rows * SLOTS * width * 2
     dma = pltpu.SemaphoreType.DMA
     edge = jax.ShapeDtypeStruct((rows, width), BF16)
-    send, sel, gas, gas_low, first, last, nu = pl.pallas_call(
+    send, sel, gas, gas_low, first, last, own_row = pl.pallas_call(
         functools.partial(pack_kernel, ng, nt),
         out_shape=(
             slab,
@@ -311,14 +319,22 @@
             jax.ShapeDtypeStruct((rows, planes, width), BF16),
             edge,
             edge,
-            jax.ShapeDtypeStruct((rows_y, planes, width), F32),
+            jax.ShapeDtypeStruct((1, 1, 128), I32),
         ),
-        in_specs=[VMEM] * 3, out_specs=(VMEM,) * 7,
+        in_specs=[VMEM] * 2, out_specs=(VMEM,) * 7,
         compiler_params=pltpu.CompilerParams(vmem_limit_bytes=slab_bytes * 2 + (6 << 20)),
         name="pack",
-    )(own_row, flow_fields, turbulent_diffusivity)
+    )(holder_unit.reshape(1, planes), flow_fields)
     halo_y = jax.ShapeDtypeStruct((nf, planes, width), BF16)
     halo_x = jax.ShapeDtypeStruct((rows, width), BF16)
+    blocks = spray_volume_position.shape[1]
+    slots = nt * SLOTS
+    prow = blocks // 128
+    bulk = (
+        patch_pick_unreduced.reshape(prow, 128), spray_volume_position[0],
+        droplet_motion[0].transpose(1, 0, 2), droplet_warmth[0], droplet_weightiness[0],
+        droplet_multiplicity[0],
+    )
     recv, ylo, yhi, xlo, xhi, own_all = pl.pallas_call(
         functools.partial(exchange_kernel, ng, nt, nf),
         out_shape=(slab, halo_y, halo_y, halo_x, halo_x, jax.ShapeDtypeStruct((nt, ng, 1, 128), I32)),
@@ -330,14 +346,17 @@
         compiler_params=pltpu.CompilerParams(collective_id=0, has_side_effects=True, vmem_limit_bytes=slab_bytes * 2 + (6 << 20)),
         name="exchange",
     )(send, gas_low, first, last, own_row)
-    blocks = spray_volume_position.shape[1]
-    slots = nt * SLOTS
-    prow = blocks // 128
     dep = pl.pallas_call(
         functools.partial(parcel_kernel, ng, nt, nf),
         out_shape=slab,
-        in_specs=[SMEM] + [VMEM] * 8, out_specs=VMEM,
+        in_specs=[SMEM] + [VMEM] * 3 + [HBM] * 5, out_specs=VMEM,
         scratch_shapes=[
+            pltpu.VMEM((blocks, 128), I32),
+            pltpu.VMEM((3, blocks, 128), F32),
+            pltpu.VMEM((blocks, 128), F32),
+            pltpu.VMEM((blocks, 128), F32),
+            pltpu.VMEM((blocks, 128), F32),
+            dma((7,)),
             pltpu.VMEM(((slots + 1) * 32, width), F32),
             pltpu.VMEM((slots + 1, 32, width), BF16),
             pltpu.VMEM(((slots + 1) * 32, width), F32),
@@ -349,12 +368,10 @@
             pltpu.SMEM((prow + 8, 128), I32),
             dma,
         ],
-        compiler_params=pltpu.CompilerParams(vmem_limit_bytes=slab_bytes * 12 + (8 << 20)),
+        compiler_params=pltpu.CompilerParams(vmem_limit_bytes=63_900_000),
         name="parcels",
     )(
-        living_spray_batches, recv, own_all.reshape(nt * ng, 128), patch_pick_unreduced.reshape(prow, 128),
-        spray_volume_position[0], droplet_motion[0].transpose(1, 0, 2), droplet_warmth[0], droplet_weightiness[0],
-        droplet_multiplicity[0],
+        living_spray_batches, recv, own_all.reshape(nt * ng, 128), *bulk,
     )
     return pl.pallas_call(
         functools.partial(finish_kernel, ng, nt, nf),
@@ -366,7 +383,7 @@
         ],
         compiler_params=pltpu.CompilerParams(collective_id=1, has_side_effects=True, vmem_limit_bytes=slab_bytes * 2 + (6 << 20)),
         name="finish",
-    )(dep, sel, gas, nu, ylo, yhi, xlo, xhi)
+    )(dep, sel, gas, turbulent_diffusivity, ylo, yhi, xlo, xhi)
 
 
 def solution(mesh):

time: 49.4 us -> 44.2 us (0.89); the launches traced: 50 us -> 43.4 us
  local copies, waits for them, and re-layouts: 9.45 us -> 4.05 us
  Pallas kernels: 39.8 us -> 38.6 us
    pallas_call x1, Pallas kernels: 19.4 us -> 9.71 us  [local(): pl.pallas_call(functools.partial(finish_kernel, ng, nt, nf), out_shape=ja...]
    pallas_call x1, Pallas kernels: 5.12 us -> 13.6 us  [local(): pl.pallas_call(functools.partial(parcel_kernel, ng, nt, nf), out_shape=sl...]
    unnamed x17 -> x13, local copies, waits for them, and re-layouts: 8.79 us -> 4.05 us
    pad x1 -> x0, local copies, waits for them, and re-layouts: 0.66 us -> none  [local(): jnp.pad(holder_unit.reshape(1, 1, planes), ((0, 0), (0, 0), (0, 128 - pla...]
where the time goes in v1:
time: 44.2 us; the launch traced here: 43.4 us
  Pallas kernels  38.6 us (87%)
  local copies, waits for them, and re-layouts  4.05 us (9%)
  between operations  0.73 us (2%)
    pallas_call x1, Pallas kernels, local(): pl.pallas_call(functools.partial(exchange_kernel, ng, nt, nf), out_shape=...  14.5 us
    pallas_call x1, Pallas kernels, local(): pl.pallas_call(functools.partial(parcel_kernel, ng, nt, nf), out_shape=sl...  13.6 us
    pallas_call x1, Pallas kernels, local(): pl.pallas_call(functools.partial(finish_kernel, ng, nt, nf), out_shape=ja...  9.71 us
    unnamed x13, local copies, waits for them, and re-layouts  4.05 us

profile of v1, /device:TPU:1, one launch (start us, length us, event | category | flops | bytes accessed | tf_op | source)
XLA Modules:
  0.0 43.4 jit_solution(10447733819086029676)
XLA Ops:
  0.0 0.0 copy-start.1
  0.0 1.0 %copy-done.1 = f32[5,32,4,128]{3,2,1,0:T(4,128)S(1)} copy-done((f32[5,32,4,128]{3,2,1,0:T(4,128)S(1)}, f32[5,32,4,128]{3,2,1,0:T(4,128)}, u32[]{:S(2)}) %copy-start.1) | copy-done | bytes 327704
  1.0 0.0 copy-start.5
  1.0 0.7 %copy-done.5 = s32[1,32,1]{1,2,0:T(1,128)S(1)} copy-done((s32[1,32,1]{1,2,0:T(1,128)S(1)}, s32[1,32,1]{1,2,0:T(1,128)}, u32[]{:S(2)}) %copy-start.5) | copy-done | bytes 152
  1.6 0.8 %pack.1 = (bf16[8,160,128]{2,1,0:T(8,128)(2,1)S(1)}, bf16[64,32]{1,0:T(8,128)(2,1)S(1)}, f32[20,32,128]{2,1,0:T(8,128)S(1)}, bf16[20,32,128]{2,1,0:T(8,128)(2,1)...) custom-call(s32[1,32]{1,0:T(1,128)S(1)} %bitcast.11, ...), custom_call_target="tpu_custom_call" | custom-call | tf_op jit(solution)/shard_map/pack/pallas_call | solution.py:313
  2.5 14.5 %exchange.1 = (bf16[8,160,128]{2,1,0:T(8,128)(2,1)S(1)}, bf16[5,32,128]{2,1,0:T(8,128)(2,1)S(1)}, bf16[5,32,128]{2,1,0:T(8,128)(2,1)S(1)}, bf16[20,128]{1,0:T(8,...) custom-call(bf16[8,160,128]{2,1,0:T(8,128)(2,1)S(1)} %get-tuple-element.18.send_ref, ...), custom_call_target="tpu_custom_call" | custom-call | tf_op jit(solution)/shard_map/exchange/pallas_call | solution.py:338
  17.0 0.0 copy-start.2
  17.0 0.7 %copy-done.2 = bf16[8,160,128]{2,1,0:T(8,128)(2,1)} copy-done((bf16[8,160,128]{2,1,0:T(8,128)(2,1)}, bf16[8,160,128]{2,1,0:T(8,128)(2,1)S(1)}, u32[]{:S(2)}) %copy-start.2) | copy-done | bytes 327704
  17.7 0.0 copy-start.4
  18.4 0.0 copy-done.4
  18.4 0.0 copy-start.3
  18.4 13.6 %parcels.1.dep_ref = bf16[8,160,128]{2,1,0:T(8,128)(2,1)} custom-call(s32[1]{0:T(128)S(6)} %copy.12.scal_ref, bf16[8,160,128]{2,1,0:T(8,128)(2,1)} %copy-done.2, s32[32,128]{1,0:T(8,128)} %bitcast.10, s32[8,128]{1,0:T(8,128)} %bitcast.17, s32[1024,128]{1,0:T(8,128)} %bitcast.13, f32[3,1024,128]{2,1,0:T(8,128)} %bitcast.12, f32[1024,128]{1,0:T(8,128)} %bitcast.14, ...), custom_call_target="tpu_custom_call" | custom-call | tf_op jit(solution)/shard_map/parcels/pallas_call | solution.py:349
  32.0 0.0 copy-done.3
  32.0 0.0 copy-start
  32.0 1.0 %copy-done = bf16[8,160,128]{2,1,0:T(8,128)(2,1)S(1)} copy-done((bf16[8,160,128]{2,1,0:T(8,128)(2,1)S(1)}, bf16[8,160,128]{2,1,0:T(8,128)(2,1)}, u32[]{:S(2)}) %copy-start) | copy-done | bytes 327704
  33.0 9.7 %finish.1 = f32[5,32,4,128]{3,2,1,0:T(4,128)S(1)} custom-call(bf16[8,160,128]{2,1,0:T(8,128)(2,1)S(1)} %copy-done, bf16[64,32]{1,0:T(8,128)(2,1)S(1)} %get-tuple-element.25.selt_ref, f32[20,32,128]{2,1,0:T(8,128)S(1)} %get-tuple-element.26.gas_ref, f32[32,4,128]{2,1,0:T(4,128)S(1)} %copy-done.3, bf16[5,32,128]{2,1,0:T(8,128)(2,1)S(1)} %get-tuple-element.27.ylo_ref, ...), custom_call_target="tpu_custom_call" | custom-call | tf_op jit(solution)/shard_map/finish/pallas_call | solution.py:376
  42.7 0.7 %copy.13 = f32[5,32,4,128]{3,2,1,0:T(4,128)} copy(f32[5,32,4,128]{3,2,1,0:T(4,128)S(1)} %finish.1) | data formatting | bytes 655360
Async XLA Ops:
  0.0 1.0 %copy-start.1 = (f32[5,32,4,128]{3,2,1,0:T(4,128)S(1)}, f32[5,32,4,128]{3,2,1,0:T(4,128)}, u32[]{:S(2)}) copy-start(f32[5,32,4,128]{3,2,1,0:T(4,128)} %flow_ref.1) | copy-start | bytes 983044
  1.0 0.7 %copy-start.5 = (s32[1,32,1]{1,2,0:T(1,128)S(1)}, s32[1,32,1]{1,2,0:T(1,128)}, u32[]{:S(2)}) copy-start(s32[1,32,1]{1,2,0:T(1,128)} %param.12) | copy-start | bytes 388
  17.0 0.7 %copy-start.2 = (bf16[8,160,128]{2,1,0:T(8,128)(2,1)}, bf16[8,160,128]{2,1,0:T(8,128)(2,1)S(1)}, u32[]{:S(2)}) copy-start(bf16[8,160,128]{2,1,0:T(8,128)(2,1)S(1)} %get-tuple-element.23.recv_ref) | copy-start | bytes 983044
  17.7 0.7 %copy-start.4 = (s32[8,4,1,128]{3,2,1,0:T(1,128)}, s32[8,4,1,128]{3,2,1,0:T(1,128)S(1)}, u32[]{:S(2)}) copy-start(s32[8,4,1,128]{3,2,1,0:T(1,128)S(1)} %get-tuple-element.24) | copy-start | bytes 49156
  18.4 13.6 %copy-start.3 = (f32[32,4,128]{2,1,0:T(4,128)S(1)}, f32[32,4,128]{2,1,0:T(4,128)}, u32[]{:S(2)}) copy-start(f32[32,4,128]{2,1,0:T(4,128)} %nu_ref.1) | copy-start | bytes 196612
  32.0 1.0 %copy-start = (bf16[8,160,128]{2,1,0:T(8,128)(2,1)S(1)}, bf16[8,160,128]{2,1,0:T(8,128)(2,1)}, u32[]{:S(2)}) copy-start(bf16[8,160,128]{2,1,0:T(8,128)(2,1)} %parcels.1.dep_ref) | copy-start | bytes 983044

commit v2 on v1

--- a/solution.py
+++ b/solution.py
@@ -9,7 +9,7 @@
 
 MESH = pl.DeviceIdType.MESH
 SLOTS = 8
-BATCH = 32
+BATCH = 64
 HBM = pl.BlockSpec(memory_space=pltpu.MemorySpace.HBM)
 VMEM = pl.BlockSpec(memory_space=pltpu.VMEM)
 SMEM = pl.BlockSpec(memory_space=pltpu.SMEM)

time: 44.2 us -> 47.9 us (1.084)
  Pallas kernels: 38.6 us -> 42.2 us
    pallas_call x1, Pallas kernels: 9.71 us -> 18.5 us  [local(): pl.pallas_call(functools.partial(finish_kernel, ng, nt, nf), out_shape=ja...]
    pallas_call x1, Pallas kernels: 13.6 us -> 8.31 us  [local(): pl.pallas_call(functools.partial(parcel_kernel, ng, nt, nf), out_shape=sl...]
where the time goes in v2:
time: 47.9 us; the launch traced here: 47 us
  Pallas kernels  42.2 us (88%)
  local copies, waits for them, and re-layouts  4.05 us (8%)
  between operations  0.73 us (2%)
    pallas_call x1, Pallas kernels, local(): pl.pallas_call(functools.partial(finish_kernel, ng, nt, nf), out_shape=ja...  18.5 us
    pallas_call x1, Pallas kernels, local(): pl.pallas_call(functools.partial(exchange_kernel, ng, nt, nf), out_shape=...  14.5 us
    pallas_call x1, Pallas kernels, local(): pl.pallas_call(functools.partial(parcel_kernel, ng, nt, nf), out_shape=sl...  8.31 us
    unnamed x13, local copies, waits for them, and re-layouts  4.05 us

profile of v2, /device:TPU:1, one launch (start us, length us, event | category | flops | bytes accessed | tf_op | source)
XLA Modules:
  0.0 47.0 jit_solution(15121569363168313398)
XLA Ops:
  0.0 0.0 copy-start.1
  0.0 1.0 %copy-done.1 = f32[5,32,4,128]{3,2,1,0:T(4,128)S(1)} copy-done((f32[5,32,4,128]{3,2,1,0:T(4,128)S(1)}, f32[5,32,4,128]{3,2,1,0:T(4,128)}, u32[]{:S(2)}) %copy-start.1) | copy-done | bytes 327704
  1.0 0.0 copy-start.5
  1.0 0.7 %copy-done.5 = s32[1,32,1]{1,2,0:T(1,128)S(1)} copy-done((s32[1,32,1]{1,2,0:T(1,128)S(1)}, s32[1,32,1]{1,2,0:T(1,128)}, u32[]{:S(2)}) %copy-start.5) | copy-done | bytes 152
  1.6 0.8 %pack.1 = (bf16[8,160,128]{2,1,0:T(8,128)(2,1)S(1)}, bf16[64,32]{1,0:T(8,128)(2,1)S(1)}, f32[20,32,128]{2,1,0:T(8,128)S(1)}, bf16[20,32,128]{2,1,0:T(8,128)(2,1)...) custom-call(s32[1,32]{1,0:T(1,128)S(1)} %bitcast.11, ...), custom_call_target="tpu_custom_call" | custom-call | tf_op jit(solution)/shard_map/pack/pallas_call | solution.py:313
  2.5 14.5 %exchange.1 = (bf16[8,160,128]{2,1,0:T(8,128)(2,1)S(1)}, bf16[5,32,128]{2,1,0:T(8,128)(2,1)S(1)}, bf16[5,32,128]{2,1,0:T(8,128)(2,1)S(1)}, bf16[20,128]{1,0:T(8,...) custom-call(bf16[8,160,128]{2,1,0:T(8,128)(2,1)S(1)} %get-tuple-element.18.send_ref, ...), custom_call_target="tpu_custom_call" | custom-call | tf_op jit(solution)/shard_map/exchange/pallas_call | solution.py:338
  17.0 0.0 copy-start.2
  17.0 0.7 %copy-done.2 = bf16[8,160,128]{2,1,0:T(8,128)(2,1)} copy-done((bf16[8,160,128]{2,1,0:T(8,128)(2,1)}, bf16[8,160,128]{2,1,0:T(8,128)(2,1)S(1)}, u32[]{:S(2)}) %copy-start.2) | copy-done | bytes 327704
  17.7 0.0 copy-start.4
  18.4 0.0 copy-done.4
  18.4 0.0 copy-start.3
  18.4 8.3 %parcels.1.dep_ref = bf16[8,160,128]{2,1,0:T(8,128)(2,1)} custom-call(s32[1]{0:T(128)S(6)} %copy.12.scal_ref, bf16[8,160,128]{2,1,0:T(8,128)(2,1)} %copy-done.2, s32[32,128]{1,0:T(8,128)} %bitcast.10, s32[8,128]{1,0:T(8,128)} %bitcast.17, s32[1024,128]{1,0:T(8,128)} %bitcast.13, f32[3,1024,128]{2,1,0:T(8,128)} %bitcast.12, f32[1024,128]{1,0:T(8,128)} %bitcast.14, ...), custom_call_target="tpu_custom_call" | custom-call | tf_op jit(solution)/shard_map/parcels/pallas_call | solution.py:349
  26.7 0.0 copy-done.3
  26.7 0.0 copy-start
  26.7 1.0 %copy-done = bf16[8,160,128]{2,1,0:T(8,128)(2,1)S(1)} copy-done((bf16[8,160,128]{2,1,0:T(8,128)(2,1)S(1)}, bf16[8,160,128]{2,1,0:T(8,128)(2,1)}, u32[]{:S(2)}) %copy-start) | copy-done | bytes 327704
  27.7 18.5 %finish.1 = f32[5,32,4,128]{3,2,1,0:T(4,128)S(1)} custom-call(bf16[8,160,128]{2,1,0:T(8,128)(2,1)S(1)} %copy-done, bf16[64,32]{1,0:T(8,128)(2,1)S(1)} %get-tuple-element.25.selt_ref, f32[20,32,128]{2,1,0:T(8,128)S(1)} %get-tuple-element.26.gas_ref, f32[32,4,128]{2,1,0:T(4,128)S(1)} %copy-done.3, bf16[5,32,128]{2,1,0:T(8,128)(2,1)S(1)} %get-tuple-element.27.ylo_ref, ...), custom_call_target="tpu_custom_call" | custom-call | tf_op jit(solution)/shard_map/finish/pallas_call | solution.py:376
  46.2 0.7 %copy.13 = f32[5,32,4,128]{3,2,1,0:T(4,128)} copy(f32[5,32,4,128]{3,2,1,0:T(4,128)S(1)} %finish.1) | data formatting | bytes 655360
Async XLA Ops:
  0.0 1.0 %copy-start.1 = (f32[5,32,4,128]{3,2,1,0:T(4,128)S(1)}, f32[5,32,4,128]{3,2,1,0:T(4,128)}, u32[]{:S(2)}) copy-start(f32[5,32,4,128]{3,2,1,0:T(4,128)} %flow_ref.1) | copy-start | bytes 983044
  1.0 0.7 %copy-start.5 = (s32[1,32,1]{1,2,0:T(1,128)S(1)}, s32[1,32,1]{1,2,0:T(1,128)}, u32[]{:S(2)}) copy-start(s32[1,32,1]{1,2,0:T(1,128)} %param.12) | copy-start | bytes 388
  17.0 0.7 %copy-start.2 = (bf16[8,160,128]{2,1,0:T(8,128)(2,1)}, bf16[8,160,128]{2,1,0:T(8,128)(2,1)S(1)}, u32[]{:S(2)}) copy-start(bf16[8,160,128]{2,1,0:T(8,128)(2,1)S(1)} %get-tuple-element.23.recv_ref) | copy-start | bytes 983044
  17.7 0.7 %copy-start.4 = (s32[8,4,1,128]{3,2,1,0:T(1,128)}, s32[8,4,1,128]{3,2,1,0:T(1,128)S(1)}, u32[]{:S(2)}) copy-start(s32[8,4,1,128]{3,2,1,0:T(1,128)S(1)} %get-tuple-element.24) | copy-start | bytes 49156
  18.4 8.3 %copy-start.3 = (f32[32,4,128]{2,1,0:T(4,128)S(1)}, f32[32,4,128]{2,1,0:T(4,128)}, u32[]{:S(2)}) copy-start(f32[32,4,128]{2,1,0:T(4,128)} %nu_ref.1) | copy-start | bytes 196612
  26.7 1.0 %copy-start = (bf16[8,160,128]{2,1,0:T(8,128)(2,1)S(1)}, bf16[8,160,128]{2,1,0:T(8,128)(2,1)}, u32[]{:S(2)}) copy-start(bf16[8,160,128]{2,1,0:T(8,128)(2,1)} %parcels.1.dep_ref) | copy-start | bytes 983044
